TPU v7x, 32 devices: a whole 2x2x4 slice. The times are simulated.
32 devices in a mesh: ctx: 8 (over z, core), fsdp: 4 (over y, x).
Axes of the slice: x: 2, y: 2, z: 4, core: 2. Of those that a mesh axis runs over, the one named last changes fastest.
Arguments:
- hidden_in: bfloat16 [4, 2048, 2048], P('fsdp', 'ctx'), may hold values from -6 to 6
- weight_query: bfloat16 [2048, 2048], P('fsdp'), may hold values from -0.125 to 0.125
- key_weight_matrix: bfloat16 [2048, 1024], P('fsdp'), may hold values from -0.125 to 0.125
- weight_value: bfloat16 [2048, 1024], P('fsdp'), may hold values from -0.125 to 0.125
- weight_out: bfloat16 [2048, 2048], P(None, 'fsdp'), may hold values from -0.5 to 0.5
- weight_gate: bfloat16 [2048, 6144], P('fsdp'), may hold values from -0.125 to 0.125
- weight_up: bfloat16 [2048, 6144], P('fsdp'), may hold values from -0.125 to 0.125
- weight_down: bfloat16 [6144, 2048], P(None, 'fsdp'), may hold values from -0.078125 to 0.078125
- gain_attention: bfloat16 [2048], P('fsdp'), may hold values from 0.5 to 1.5
- gain_feed: bfloat16 [2048], P('fsdp'), may hold values from 0.5 to 1.5
- gain_query: bfloat16 [128], P('fsdp'), may hold values from 0.25 to 1.75
- gain_key: bfloat16 [128], P('fsdp'), may hold values from 0.25 to 1.75
- positions: int32 [4, 2048], P('fsdp', 'ctx'), may hold values from 0 to 4095
- token_block_index: int32 [4, 2048], P('fsdp', 'ctx'), may hold values from 0 to 15, never falling along the last dimension, each value on 1 to 256 neighbouring positions
- grad_out: bfloat16 [4, 2048, 2048], P('fsdp', 'ctx'), may hold values from -6 to 6
Outputs:
- hidden_out: bfloat16 [4, 2048, 2048], P('fsdp', 'ctx')
- grad_hidden: float32 [4, 2048, 2048], P('fsdp', 'ctx')
- grad_weight_query: float32 [2048, 2048], P('fsdp')
- grad_weight_key: float32 [2048, 1024], P('fsdp')
- grad_weight_value: float32 [2048, 1024], P('fsdp')
- grad_weight_out: float32 [2048, 2048], P(None, 'fsdp')
- grad_weight_gate: float32 [2048, 6144], P('fsdp')
- grad_weight_up: float32 [2048, 6144], P('fsdp')
- grad_weight_down: float32 [6144, 2048], P(None, 'fsdp')
- grad_gain_attention: float32 [2048], P('fsdp')
- grad_gain_feed: float32 [2048], P('fsdp')
- grad_gain_query: float32 [128], P('fsdp')
- grad_gain_key: float32 [128], P('fsdp')
Inputs may be any that keep to these rules, and one draw needn't show every extreme that they name: `token_block_index`: within each sequence the block ids never fall; each block holds 1 to 256 consecutive tokens and one holds exactly 256.
All inputs are finite; a program needn't handle non-finite values.
Results may differ from a plain program's by a relative error of at most 0.025.
Values may be sent and summed in bfloat16 or wider, within the bound.
A program may use at most 640 MiB of HBM per device.

v0:
```python
import jax
import jax.numpy as jnp
from jax import lax
from jax.sharding import PartitionSpec as P

D = 2048
QUERY_HEADS = 16
KEY_VALUE_HEADS = 8
HEAD_SIZE = 128
FF = 6144
EPS = 1e-06
THETA = 1000000.0
NEGATIVE_LARGE = -1e30


def from_behind(shard, axis, by):
    peers = lax.axis_size(axis)
    return lax.ppermute(shard, axis, [(i, (i + by) % peers) for i in range(peers)])


def tdot(left, right):
    return lax.dot_general(
        left, right, (((0,), (0,)), ((), ())), preferred_element_type=jnp.float32
    )


def rdot(left, right):
    return lax.dot_general(
        left, right, (((1,), (1,)), ((), ())), preferred_element_type=jnp.float32
    )


def tables(positions):
    half = HEAD_SIZE // 2
    freq = THETA ** (-(jnp.arange(half).astype(jnp.float32) * 2.0 / HEAD_SIZE))
    angle = positions.astype(jnp.float32)[..., None] * freq
    return (jnp.cos(angle), jnp.sin(angle))


def rotary(value, cosine_table, sine_table):
    half = value.shape[-1] // 2
    first = value[..., :half]
    second = value[..., half:]
    return jnp.concatenate(
        [first * cosine_table - second * sine_table, second * cosine_table + first * sine_table],
        axis=-1,
    )


def reverse_rotation(grad, cosine_table, sine_table):
    half = grad.shape[-1] // 2
    first = grad[..., :half]
    second = grad[..., half:]
    return jnp.concatenate(
        [first * cosine_table + second * sine_table, second * cosine_table - first * sine_table],
        axis=-1,
    )


def rms_forward(value, gain):
    inverse = lax.rsqrt(jnp.mean(value * value, axis=-1, keepdims=True) + EPS)
    return (value * inverse * gain, inverse)


def rms_backward(value, inverse, gain, grad):
    scaled = grad * gain
    inner = jnp.mean(scaled * value, axis=-1, keepdims=True)
    return (inverse * scaled - value * inverse * inverse * inverse * inner, grad * value * inverse)


def local(
    hidden_in,
    weight_query,
    key_weight_matrix,
    weight_value,
    weight_out,
    weight_gate,
    weight_up,
    weight_down,
    gain_attention,
    gain_feed,
    gain_query,
    gain_key,
    positions,
    token_block_index,
    grad_out,
):
    gathered = (
        lax.all_gather(weight_query, "fsdp", axis=0, tiled=True),
        lax.all_gather(key_weight_matrix, "fsdp", axis=0, tiled=True),
        lax.all_gather(weight_value, "fsdp", axis=0, tiled=True),
        lax.all_gather(weight_out, "fsdp", axis=1, tiled=True),
        lax.all_gather(weight_gate, "fsdp", axis=0, tiled=True),
        lax.all_gather(weight_up, "fsdp", axis=0, tiled=True),
        lax.all_gather(weight_down, "fsdp", axis=1, tiled=True),
        lax.all_gather(gain_attention, "fsdp", axis=0, tiled=True),
        lax.all_gather(gain_feed, "fsdp", axis=0, tiled=True),
        lax.all_gather(gain_query, "fsdp", axis=0, tiled=True),
        lax.all_gather(gain_key, "fsdp", axis=0, tiled=True),
    )
    full_query, full_key, full_value, full_out, full_gate, full_up, full_down = gathered[:7]
    norm_attention = gathered[7].astype(jnp.float32)
    norm_feed = gathered[8].astype(jnp.float32)
    norm_query = gathered[9].astype(jnp.float32)
    norm_key = gathered[10].astype(jnp.float32)
    residual = hidden_in.reshape(-1, D).astype(jnp.float32)
    local_row_count = residual.shape[0]
    query_group = QUERY_HEADS // KEY_VALUE_HEADS
    scale = HEAD_SIZE ** (-0.5)
    key_total_width = KEY_VALUE_HEADS * HEAD_SIZE
    cosine_table, sine_table = tables(positions.reshape(-1))
    cosine_table = cosine_table[:, None, :]
    sine_table = sine_table[:, None, :]
    query_ids = token_block_index.reshape(-1)
    key_ids = lax.all_gather(token_block_index, "ctx", axis=1, tiled=True).reshape(-1)
    normed, inverse_one = rms_forward(residual, norm_attention)
    normed_low = normed.astype(jnp.bfloat16)
    query_proj = jnp.dot(normed_low, full_query, preferred_element_type=jnp.float32).reshape(
        local_row_count, QUERY_HEADS, HEAD_SIZE
    )
    query_normed, inverse_query = rms_forward(query_proj, norm_query)
    query_matrix = (
        (rotary(query_normed, cosine_table, sine_table) * scale)
        .astype(jnp.bfloat16)
        .reshape(local_row_count, KEY_VALUE_HEADS, query_group, HEAD_SIZE)
    )
    key_projected = jnp.dot(normed_low, full_key, preferred_element_type=jnp.float32).reshape(
        local_row_count, KEY_VALUE_HEADS, HEAD_SIZE
    )
    key_normed, inverse_key = rms_forward(key_projected, norm_key)
    key_row_values = (
        rotary(key_normed, cosine_table, sine_table)
        .astype(jnp.bfloat16)
        .reshape(local_row_count, key_total_width)
    )
    value_row_values = jnp.dot(normed_low, full_value, preferred_element_type=jnp.float32).astype(
        jnp.bfloat16
    )
    portion_keys = lax.all_gather(key_row_values, "ctx", axis=0, tiled=True)
    portion_values = lax.all_gather(value_row_values, "ctx", axis=0, tiled=True)
    token_count = portion_keys.shape[0]
    piece_ids = key_ids
    previous_maximum = jnp.full(
        (local_row_count, KEY_VALUE_HEADS, query_group), NEGATIVE_LARGE, jnp.float32
    )
    scores = jnp.einsum(
        "qgrd,kgd->qgrk",
        query_matrix,
        portion_keys.reshape(token_count, KEY_VALUE_HEADS, HEAD_SIZE),
        preferred_element_type=jnp.float32,
    )
    allowed = (piece_ids[None, :] <= query_ids[:, None])[:, None, None, :]
    masked = jnp.where(allowed, scores, NEGATIVE_LARGE)
    new_max = jnp.maximum(previous_maximum, jnp.max(masked, axis=-1))
    weights = jnp.where(allowed, jnp.exp(masked - new_max[..., None]), 0.0)
    new_sum = jnp.sum(weights, axis=-1)
    new_acc = jnp.einsum(
        "qgrk,kgd->qgrd",
        weights.astype(jnp.bfloat16),
        portion_values.reshape(token_count, KEY_VALUE_HEADS, HEAD_SIZE),
        preferred_element_type=jnp.float32,
    )
    log_total = new_max + jnp.log(new_sum)
    context = (
        (new_acc / new_sum[..., None])
        .reshape(local_row_count, QUERY_HEADS * HEAD_SIZE)
        .astype(jnp.bfloat16)
    )
    middle = residual + jnp.dot(context, full_out, preferred_element_type=jnp.float32)
    normed_two, inverse_two = rms_forward(middle, norm_feed)
    normed_two_low = normed_two.astype(jnp.bfloat16)
    gate_proj = jnp.dot(normed_two_low, full_gate, preferred_element_type=jnp.float32)
    up_proj = jnp.dot(normed_two_low, full_up, preferred_element_type=jnp.float32)
    sigma = jax.nn.sigmoid(gate_proj)
    activation = (gate_proj * sigma * up_proj).astype(jnp.bfloat16)
    hidden_out = (
        middle + jnp.dot(activation, full_down, preferred_element_type=jnp.float32)
    ).astype(jnp.bfloat16)
    grad_low = grad_out.reshape(local_row_count, D)
    grad_act = rdot(grad_low, full_down)
    grad_gate = (grad_act * up_proj * sigma * (1.0 + gate_proj * (1.0 - sigma))).astype(
        jnp.bfloat16
    )
    grad_upward = (grad_act * gate_proj * sigma).astype(jnp.bfloat16)
    fsdp_count = lax.axis_size("fsdp")
    shard_rows = D // fsdp_count
    select = lambda array: array
    picked = select(normed_two_low)
    feed_shard = lax.psum_scatter(
        jnp.concatenate(
            [
                tdot(picked, grad_gate),
                tdot(picked, grad_upward),
                tdot(select(grad_low), activation),
            ],
            axis=1,
        ).astype(jnp.bfloat16),
        "fsdp",
        scatter_dimension=0,
        tiled=True,
    ).astype(jnp.float32)
    grad_normed_two = rdot(grad_gate, full_gate) + rdot(grad_upward, full_up)
    back_two, gain_two_terms = rms_backward(middle, inverse_two, norm_feed, grad_normed_two)
    grad_middle = grad_low.astype(jnp.float32) + back_two
    grad_attention = grad_middle.astype(jnp.bfloat16)
    context_gradient = rdot(grad_attention, full_out).astype(jnp.bfloat16)
    context_head_gradient = context_gradient.reshape(
        local_row_count, KEY_VALUE_HEADS, query_group, HEAD_SIZE
    )
    delta = jnp.sum(
        (context_gradient.astype(jnp.float32) * context.astype(jnp.float32)).reshape(
            local_row_count, KEY_VALUE_HEADS, query_group, HEAD_SIZE
        ),
        axis=-1,
    )
    own_index = lax.axis_index("ctx")
    cycle_size = lax.axis_size("ctx")

    def cycle_step(step_index, state):
        rotating_keys, rotating_values, key_gradient, grad_values, grad_queries = state
        source = (own_index - step_index) % cycle_size
        piece_ids = lax.dynamic_slice_in_dim(key_ids, source * local_row_count, local_row_count)
        acc_keys = key_gradient
        acc_values = grad_values
        acc_queries = grad_queries
        key_head_rows = rotating_keys.reshape(local_row_count, KEY_VALUE_HEADS, HEAD_SIZE)
        value_head_rows = rotating_values.reshape(local_row_count, KEY_VALUE_HEADS, HEAD_SIZE)
        scores = jnp.einsum(
            "qgrd,kgd->qgrk", query_matrix, key_head_rows, preferred_element_type=jnp.float32
        )
        allowed = (piece_ids[None, :] <= query_ids[:, None])[:, None, None, :]
        probs = jnp.where(
            allowed, jnp.exp(jnp.where(allowed, scores, NEGATIVE_LARGE) - log_total[..., None]), 0.0
        )
        grad_probs = jnp.einsum(
            "qgrd,kgd->qgrk",
            context_head_gradient,
            value_head_rows,
            preferred_element_type=jnp.float32,
        )
        grad_scores = (probs * (grad_probs - delta[..., None])).astype(jnp.bfloat16)
        acc_values = acc_values + jnp.einsum(
            "qgrk,qgrd->kgd",
            probs.astype(jnp.bfloat16),
            context_head_gradient,
            preferred_element_type=jnp.float32,
        ).reshape(local_row_count, key_total_width)
        acc_keys = acc_keys + jnp.einsum(
            "qgrk,qgrd->kgd", grad_scores, query_matrix, preferred_element_type=jnp.float32
        ).reshape(local_row_count, key_total_width)
        acc_queries = acc_queries + jnp.einsum(
            "qgrk,kgd->qgrd", grad_scores, key_head_rows, preferred_element_type=jnp.float32
        )
        rotating_keys, rotating_values = from_behind((rotating_keys, rotating_values), "ctx", 1)
        key_gradient, grad_values = (
            from_behind(acc_keys.astype(jnp.bfloat16), "ctx", 1).astype(jnp.float32),
            from_behind(acc_values.astype(jnp.bfloat16), "ctx", 1).astype(jnp.float32),
        )
        return (rotating_keys, rotating_values, key_gradient, grad_values, acc_queries)

    cycle_start = (
        key_row_values,
        value_row_values,
        jnp.zeros((local_row_count, key_total_width), jnp.float32),
        jnp.zeros((local_row_count, key_total_width), jnp.float32),
        jnp.zeros((local_row_count, KEY_VALUE_HEADS, query_group, HEAD_SIZE), jnp.float32),
    )
    cycle_final = lax.fori_loop(0, cycle_size, cycle_step, cycle_start)
    key_gradient, grad_values, grad_queries = (cycle_final[2], cycle_final[3], cycle_final[4])
    query_back = reverse_rotation(
        grad_queries.reshape(local_row_count, QUERY_HEADS, HEAD_SIZE) * scale,
        cosine_table,
        sine_table,
    )
    back_query, query_gain_terms = rms_backward(query_proj, inverse_query, norm_query, query_back)
    grad_query_low = back_query.reshape(local_row_count, QUERY_HEADS * HEAD_SIZE).astype(
        jnp.bfloat16
    )
    key_backward = reverse_rotation(
        key_gradient.reshape(local_row_count, KEY_VALUE_HEADS, HEAD_SIZE), cosine_table, sine_table
    )
    back_key, key_gain_terms = rms_backward(key_projected, inverse_key, norm_key, key_backward)
    grad_key_low = back_key.reshape(local_row_count, key_total_width).astype(jnp.bfloat16)
    grad_value_low = grad_values.astype(jnp.bfloat16)
    grad_normed_one = (
        rdot(grad_query_low, full_query)
        + rdot(grad_key_low, full_key)
        + rdot(grad_value_low, full_value)
    )
    back_one, gain_one_terms = rms_backward(residual, inverse_one, norm_attention, grad_normed_one)
    grad_hidden = (grad_middle + back_one).reshape(hidden_in.shape)
    select = lambda array: array
    picked = select(normed_low)
    attention_shard = lax.psum_scatter(
        jnp.concatenate(
            [
                tdot(picked, grad_query_low),
                tdot(picked, grad_key_low),
                tdot(picked, grad_value_low),
                tdot(select(grad_attention), context),
            ],
            axis=1,
        ).astype(jnp.bfloat16),
        "fsdp",
        scatter_dimension=0,
        tiled=True,
    ).astype(jnp.float32)
    attention_shard, feed_shard = (
        lax.psum(attention_shard.astype(jnp.bfloat16), "ctx").astype(jnp.float32),
        lax.psum(feed_shard.astype(jnp.bfloat16), "ctx").astype(jnp.float32),
    )
    gain_totals = lax.psum(
        (
            jnp.sum(gain_one_terms, axis=0),
            jnp.sum(gain_two_terms, axis=0),
            jnp.sum(query_gain_terms, axis=(0, 1)),
            jnp.sum(key_gain_terms, axis=(0, 1)),
        ),
        ("ctx", "fsdp"),
    )
    fsdp_index = lax.axis_index("fsdp")
    head_rows = HEAD_SIZE // fsdp_count
    query_width = QUERY_HEADS * HEAD_SIZE
    grad_gain_attention = lax.dynamic_slice_in_dim(
        gain_totals[0], fsdp_index * shard_rows, shard_rows
    )
    grad_gain_feed = lax.dynamic_slice_in_dim(gain_totals[1], fsdp_index * shard_rows, shard_rows)
    grad_gain_query = lax.dynamic_slice_in_dim(gain_totals[2], fsdp_index * head_rows, head_rows)
    grad_gain_key = lax.dynamic_slice_in_dim(gain_totals[3], fsdp_index * head_rows, head_rows)
    grad_weight_query = attention_shard[:, :query_width]
    grad_weight_key = attention_shard[:, query_width : query_width + key_total_width]
    grad_weight_value = attention_shard[
        :, query_width + key_total_width : query_width + 2 * key_total_width
    ]
    grad_weight_out = attention_shard[:, query_width + 2 * key_total_width :].T
    grad_weight_gate = feed_shard[:, :FF]
    grad_weight_up = feed_shard[:, FF : 2 * FF]
    grad_weight_down = feed_shard[:, 2 * FF :].T
    return (
        hidden_out.reshape(hidden_in.shape),
        grad_hidden,
        grad_weight_query,
        grad_weight_key,
        grad_weight_value,
        grad_weight_out,
        grad_weight_gate,
        grad_weight_up,
        grad_weight_down,
        grad_gain_attention,
        grad_gain_feed,
        grad_gain_query,
        grad_gain_key,
    )


def solution(mesh):
    return jax.shard_map(
        local,
        mesh=mesh,
        in_specs=(
            P("fsdp", "ctx", None),
            P("fsdp", None),
            P("fsdp", None),
            P("fsdp", None),
            P(None, "fsdp"),
            P("fsdp", None),
            P("fsdp", None),
            P(None, "fsdp"),
            P("fsdp"),
            P("fsdp"),
            P("fsdp"),
            P("fsdp"),
            P("fsdp", "ctx"),
            P("fsdp", "ctx"),
            P("fsdp", "ctx", None),
        ),
        out_specs=(
            P("fsdp", "ctx", None),
            P("fsdp", "ctx", None),
            P("fsdp", None),
            P("fsdp", None),
            P("fsdp", None),
            P(None, "fsdp"),
            P("fsdp", None),
            P("fsdp", None),
            P(None, "fsdp"),
            P("fsdp"),
            P("fsdp"),
            P("fsdp"),
            P("fsdp"),
        ),
        check_vma=False,
    )
```

profile of v0, /device:TPU:0, one launch (start us, length us, event | category | flops | bytes accessed | tf_op | source)
XLA Modules:
  0.0 2910.7 jit_solution(13086285690502229014)
XLA Ops:
  19.3 46.0 %all-gather.12.cloned.1.call-done = bf16[2048,1024]{1,0:T(8,128)(2,1)} async-done(((bf16[512,1024]{1,0:T(8,128)(2,1)}), bf16[2048,1024]{1,0:T(8,128)(2,1)}) %all-gather.12.cloned.1.call-update) | async-done | bytes 4194320 | tf_op jit(solution)/shard_map/all_gather | solution.py:91
  80.9 39.0 %all-gather.16.cloned.1.call-done = bf16[2048,1024]{1,0:T(8,128)(2,1)} async-done(((bf16[512,1024]{1,0:T(8,128)(2,1)}), bf16[2048,1024]{1,0:T(8,128)(2,1)}) %all-gather.16.cloned.1.call-update) | async-done | bytes 4194320 | tf_op jit(solution)/shard_map/all_gather | solution.py:90
  143.1 12.2 all_gather.45
  156.8 52.6 %all-gather.20.cloned.1.call-done = bf16[2048,2048]{1,0:T(8,128)(2,1)} async-done(((bf16[512,2048]{1,0:T(8,128)(2,1)}), bf16[2048,2048]{1,0:T(8,128)(2,1)}) %all-gather.20.cloned.1.call-update) | async-done | bytes 8388624 | tf_op jit(solution)/shard_map/all_gather | solution.py:89
  209.5 12.3 copy.86
  238.7 19.4 all-gather.14.cloned.1.call-done
  264.5 42.1 %all-gather.18.cloned.1.call-done = bf16[2048,1024]{0,1:T(8,128)(2,1)} async-done(((bf16[256,1024]{0,1:T(8,128)(2,1)}), bf16[2048,1024]{0,1:T(8,128)(2,1)}) %all-gather.18.cloned.1.call-update) | async-done | bytes 4194320 | tf_op jit(solution)/shard_map/all_gather | solution.py:139
  306.7 17.4 fusion.20
  324.1 14.3 fusion.21
  338.4 15.8 fusion.48
  355.6 38.4 %all-gather.22.cloned.1.call-done = bf16[2048,2048]{1,0:T(8,128)(2,1)} async-done(((bf16[2048,512]{1,0:T(8,128)(2,1)}), bf16[2048,2048]{1,0:T(8,128)(2,1)}) %all-gather.22.cloned.1.call-update) | async-done | bytes 8388624 | tf_op jit(solution)/shard_map/all_gather | solution.py:92
  400.5 223.2 %all-gather.26.cloned.1.call-done = bf16[2048,6144]{1,0:T(8,128)(2,1)} async-done(((bf16[512,6144]{1,0:T(8,128)(2,1)}), bf16[2048,6144]{1,0:T(8,128)(2,1)}) %all-gather.26.cloned.1.call-update) | async-done | bytes 25165840 | tf_op jit(solution)/shard_map/all_gather | solution.py:94
  623.7 15.5 fusion.76
  639.2 214.1 %all-gather.24.cloned.1.call-done = bf16[2048,6144]{1,0:T(8,128)(2,1)} async-done(((bf16[512,6144]{1,0:T(8,128)(2,1)}), bf16[2048,6144]{1,0:T(8,128)(2,1)}) %all-gather.24.cloned.1.call-update) | async-done | bytes 25165840 | tf_op jit(solution)/shard_map/all_gather | solution.py:93
  853.3 15.5 fusion.75
  868.8 214.0 %all-gather.28.cloned.1.call-done = bf16[6144,2048]{1,0:T(8,128)(2,1)} async-done(((bf16[6144,512]{1,0:T(8,128)(2,1)}), bf16[6144,2048]{1,0:T(8,128)(2,1)}) %all-gather.28.cloned.1.call-update) | async-done | bytes 25165840 | tf_op jit(solution)/shard_map/all_gather | solution.py:95
  1082.8 20.6 multiply_convert_fusion
  1103.4 13.5 fusion.77
  1116.8 15.1 multiply_reduce_fusion.1
  1155.2 283.0 %while.24 = (s32[]{:T(128)}, bf16[256,1024]{1,0:T(8,128)(2,1)}, bf16[256,1024]{1,0:T(8,128)(2,1)}, f32[256,1024]{0,1:T(8,128)}, f32[256,1024]{0,1:T(8,128)S(1)},...) while((s32[]{:T(128)}, bf16[256,1024]{1,0:T(8,128)(2,1)}, ...), condition=%wide.region_9.10_spmd.clone, body=%wide.region_8.9_spmd.clone.sunk | while | flops 1355874304 | bytes 62640716 | solution.py:268
  1463.1 18.0 pad_maximum_fusion.1
  1481.2 14.1 convert_bitcast_fusion
  1495.3 14.0 convolution_convert_fusion
  1509.2 14.3 convolution_convert_fusion.1
  1523.5 51.4 %pad_maximum_fusion = bf16[2048,18432]{1,0:T(8,128)(2,1)} fusion(bf16[2048,6144]{1,0:T(8,128)(2,1)} %convert_bitcast_fusion, bf16[2048,6144]{1,0:T(8,128)(2,1)} %convolution_convert_fusion, bf16[2048,6144]{1,0:T(8,128)(2,1)} %convolution_convert_fusion.1), kind=kLoop, calls=%fused_computation.25 | loop fusion | flops 226492416 | bytes 150994944 | tf_op jit(solution)/shard_map/concatenate | solution.py:190
  1575.3 125.1 %reduce-scatter.5.cloned.1.call-done = bf16[512,6144]{0,1:T(8,128)(2,1)} async-done(((bf16[2048,6144]{0,1:T(8,128)(2,1)}), bf16[512,6144]{0,1:T(8,128)(2,1)}) %reduce-scatter.5.cloned.1.call-update) | async-done | bytes 6291472 | tf_op jit(solution)/shard_map/reduce_scatter | solution.py:294
  1700.4 629.3 %reduce-scatter.7.cloned.1.call-done = bf16[512,18432]{1,0:T(8,128)(2,1)} async-done(((bf16[2048,18432]{1,0:T(8,128)(2,1)}), bf16[512,18432]{1,0:T(8,128)(2,1)}) %reduce-scatter.7.cloned.1.call-update) | async-done | bytes 18874384
  2342.0 40.7 %all-reduce.3 = (f32[2048]{0:T(1024)S(1)}, f32[2048]{0:T(1024)S(1)}, f32[128]{0:T(128)S(1)}, f32[128]{0:T(128)S(1)}) all-reduce(f32[2048]{0:T(1024)S(1)} %get-tuple-element.451, f32[2048]{0:T(1024)S(1)} %copy-done.41, f32[128]{0:T(128)S(1)} %get-tuple-element.447, ...), channel_id=1, replica_groups=mesh['ctx'=8,'fsdp'=4] {'ctx','fsdp'}, use_global_device_ids=true, to_apply=%region_18.19 | all-reduce | flops 4352 | bytes 34816 | tf_op jit(solution)/shard_map/psum | solution.py:312
  2389.7 13.0 fusion.34
  2402.7 421.8 %all-reduce.8.cloned.1.call-done = (bf16[512,6144]{0,1:T(8,128)(2,1)}, bf16[512,18432]{1,0:T(8,128)(2,1)}) async-done(((bf16[512,6144]{0,1:T(8,128)(2,1)}, bf16[512,18432]{1,0:T(8,128)(2,1)}), (bf16[512,6144]{0,1:T(8,128)(2,1)}, bf16[512,18432]{1,0:T(8,128)(2,1)})) %all-reduce.8.cloned.1.call-update) | async-done | bytes 25165840 | tf_op jit(solution)/shard_map/psum | solution.py:309
  2852.4 13.0 convert_element_type.227
  2890.8 12.6 copy.102
  (455 shorter events, 484.9 us)
Async XLA Ops:
  7.2 58.1 %all-gather.12.cloned.1.call-start = ((), (), s32[]{:S(2)}) async-start(), calls=%async_computation.2 | async-start | bytes 5242880 | tf_op jit(solution)/shard_map/all_gather | solution.py:91
  7.9 112.0 %all-gather.16.cloned.1.call-start = ((), (), s32[]{:S(2)}) async-start(), calls=%async_computation.4 | async-start | bytes 5242880 | tf_op jit(solution)/shard_map/all_gather | solution.py:90
  8.7 200.8 %all-gather.20.cloned.1.call-start = ((), (), s32[]{:S(2)}) async-start(), calls=%async_computation.6 | async-start | bytes 10485760 | tf_op jit(solution)/shard_map/all_gather | solution.py:89
  9.4 248.7 %all-gather.14.cloned.1.call-start = ((), (), s32[]{:S(2)}) async-start(), calls=%async_computation.3 | async-start | bytes 4718592 | tf_op jit(solution)/shard_map/all_gather | solution.py:140
  69.7 237.0 %all-gather.18.cloned.1.call-start = ((), (), s32[]{:S(2)}) async-start(), calls=%async_computation.5 | async-start | bytes 4718592 | tf_op jit(solution)/shard_map/all_gather | solution.py:139
  132.3 261.8 %all-gather.22.cloned.1.call-start = ((), (), s32[]{:S(2)}) async-start(), calls=%async_computation.7 | async-start | bytes 10485760 | tf_op jit(solution)/shard_map/all_gather | solution.py:92
  132.9 490.8 %all-gather.26.cloned.1.call-start = ((), (), s32[]{:S(2)}) async-start(), calls=%async_computation.9 | async-start | bytes 31457280 | tf_op jit(solution)/shard_map/all_gather | solution.py:94
  133.6 719.7 %all-gather.24.cloned.1.call-start = ((), (), s32[]{:S(2)}) async-start(), calls=%async_computation.8 | async-start | bytes 31457280 | tf_op jit(solution)/shard_map/all_gather | solution.py:93
  134.4 948.4 %all-gather.28.cloned.1.call-start = ((), (), s32[]{:S(2)}) async-start(), calls=%async_computation.10 | async-start | bytes 31457280 | tf_op jit(solution)/shard_map/all_gather | solution.py:95
  135.2 1565.2 %reduce-scatter.5.cloned.1.call-start = ((), (), s32[]{:S(2)}) async-start(), calls=%async_computation.11 | async-start | bytes 31457280 | tf_op jit(solution)/shard_map/reduce_scatter | solution.py:294
  1162.5 13.0 collective-permute-start.3
  1170.7 14.7 collective-permute-start
  1170.7 20.3 collective-permute-start.1
  1197.8 11.9 collective-permute-start.3
  1204.4 10.7 collective-permute-start.2
  1204.4 16.3 collective-permute-start
  1204.4 21.9 collective-permute-start.1
  1239.7 10.7 collective-permute-start.2
  1239.7 16.3 collective-permute-start
  1239.7 21.9 collective-permute-start.1
  1275.0 16.3 collective-permute-start
  1275.0 21.9 collective-permute-start.1
  1310.3 16.3 collective-permute-start
  1310.3 21.9 collective-permute-start.1
  1345.7 16.3 collective-permute-start
  1345.7 21.9 collective-permute-start.1
  1381.0 16.3 collective-permute-start
  1381.0 21.9 collective-permute-start.1
  1416.3 16.3 collective-permute-start
  1416.3 21.9 collective-permute-start.1
  1481.1 848.6 %reduce-scatter.7.cloned.1.call-start = ((), (), s32[]{:S(2)}) async-start(), calls=%async_computation.12 | async-start | bytes 94371840
  1575.0 1249.5 %all-reduce.8.cloned.1.call-start = ((), (), s32[]{:S(2)}) async-start(), calls=%async_computation.13 | async-start | bytes 50331648 | tf_op jit(solution)/shard_map/psum | solution.py:309
  (92 other events, 3672.6 us)
Sparse Core Ops, SparseCore 0:
  9.9 55.3 all-gather.11
  67.2 52.6 all-gather.15
  121.7 87.6 all-gather.19
  210.9 47.1 all-gather.13
  260.1 46.5 all-gather.17
  308.3 85.6 all-gather.21
  395.9 227.7 all-gather.25
  625.6 227.7 all-gather.23
  855.2 227.5 all-gather.27
  1481.2 219.1 reduce-scatter.4
  1703.8 625.8 reduce-scatter.6
  2332.2 492.2 all-reduce.7
where the time goes:
time: 2920 us; the launch traced here: 2910 us
  waiting for transfers between devices  2180 us (75%)
  matrix products  284 us (10%)
  other arithmetic  175 us (6%)
  local copies, waits for them, and re-layouts  165 us (6%)
  blocking collectives  79.3 us (3%)
    unnamed x13, waiting for transfers between devices  634 us
    psum x1, waiting for transfers between devices, local(): lax.psum(attention_shard.astype(jnp.bfloat16), 'ctx').astype(jnp.float32)  422 us
    all_gather x1, waiting for transfers between devices, local(): lax.all_gather(weight_up, 'fsdp', axis=0, tiled=True)  223 us
    all_gather x1, waiting for transfers between devices, local(): lax.all_gather(weight_gate, 'fsdp', axis=0, tiled=True)  214 us
    all_gather x1, waiting for transfers between devices, local(): lax.all_gather(weight_down, 'fsdp', axis=1, tiled=True)  214 us
    reduce_scatter x1, waiting for transfers between devices, local(): lax.psum_scatter(jnp.concatenate([tdot(picked, grad_query_low), tdot(pick...  125 us
    ppermute x32, waiting for transfers between devices, from_behind(): lax.ppermute(shard, axis, [(i, (i + by) % peers) for i in range(peers)])  114 us
    dot_general x7, matrix products, rdot(): lax.dot_general(left, right, (((1,), (1,)), ((), ())), preferred_element_...  63.1 us
  transfers between devices with their start and end apart: 44, of which 42 were waited for; matrix products, arithmetic and copies ran while one was open for 13% of the time, Pallas kernels for 0%

commit v1 on v0

--- a/solution.py
+++ b/solution.py
@@ -11,6 +11,19 @@
 EPS = 1e-06
 THETA = 1000000.0
 NEGATIVE_LARGE = -1e30
+
+
+def ring_gather(value, axis, dim):
+    ways = lax.axis_size(axis)
+    up = [(d, (d + 1) % ways) for d in range(ways)]
+    down = [(d, (d - 1) % ways) for d in range(ways)]
+    earlier, later = ([value], [value])
+    for _ in range(ways // 2):
+        earlier.append(lax.ppermute(earlier[-1], axis, up))
+    for _ in range((ways - 1) // 2):
+        later.append(lax.ppermute(later[-1], axis, down))
+    line = jnp.concatenate([*earlier[::-1], *later[1:]], axis=dim)
+    return jnp.roll(line, (lax.axis_index(axis) - ways // 2) * value.shape[dim], axis=dim)
 
 
 def from_behind(shard, axis, by):
@@ -90,7 +103,7 @@
         lax.all_gather(key_weight_matrix, "fsdp", axis=0, tiled=True),
         lax.all_gather(weight_value, "fsdp", axis=0, tiled=True),
         lax.all_gather(weight_out, "fsdp", axis=1, tiled=True),
-        lax.all_gather(weight_gate, "fsdp", axis=0, tiled=True),
+        ring_gather(weight_gate, "fsdp", 0),
         lax.all_gather(weight_up, "fsdp", axis=0, tiled=True),
         lax.all_gather(weight_down, "fsdp", axis=1, tiled=True),
         lax.all_gather(gain_attention, "fsdp", axis=0, tiled=True),

time: 2920 us -> 3020 us (1.034)
  blocking collectives: 79.3 us -> 479 us
  waiting for transfers between devices: 2180 us -> 1800 us
  local copies, waits for them, and re-layouts: 165 us -> 218 us
    all_gather x1, blocking collectives: 7.83 us -> 407 us  [local(): lax.all_gather(gain_feed, 'fsdp', axis=0, tiled=True)]
    all_gather x1, waiting for transfers between devices: 223 us -> 0.02 us  [local(): lax.all_gather(weight_up, 'fsdp', axis=0, tiled=True)]
    all_gather x1 -> x0, waiting for transfers between devices: 214 us -> none  [local(): lax.all_gather(weight_gate, 'fsdp', axis=0, tiled=True)]
    ppermute x0 -> x3, waiting for transfers between devices: none -> 201 us  [the longest x2 201 us: ring_gather(): earlier.append(lax.ppermute(earlier[-1], axis, up))]
    all_gather x1, waiting for transfers between devices: 52.6 us -> 0.01 us  [local(): lax.all_gather(weight_query, 'fsdp', axis=0, tiled=True)]
    unnamed x127 -> x136, local copies, waits for them, and re-layouts: 33.5 us -> 76.9 us
    all_gather x1, waiting for transfers between devices: 42.1 us -> 0.01 us  [local(): portion_keys = lax.all_gather(key_row_values, 'ctx', axis=0, tiled=True)]
    all_gather x1, waiting for transfers between devices: 38.4 us -> 0.01 us  [local(): lax.all_gather(weight_out, 'fsdp', axis=1, tiled=True)]
  transfers between devices with their start and end apart: 44 -> 46, of which waited for: 42 -> 39; matrix products, arithmetic and copies ran while one was open for 13% -> 13% of each run, Pallas kernels for 0% -> 0%
where the time goes in v1:
time: 3020 us; the launch traced here: 3010 us
  waiting for transfers between devices  1800 us (60%)
  blocking collectives  479 us (16%)
  matrix products  297 us (10%)
  local copies, waits for them, and re-layouts  218 us (7%)
  other arithmetic  186 us (6%)
    unnamed x12, waiting for transfers between devices  633 us
    psum x1, waiting for transfers between devices, local(): lax.psum(attention_shard.astype(jnp.bfloat16), 'ctx').astype(jnp.float32)  420 us
    all_gather x1, blocking collectives, local(): lax.all_gather(gain_feed, 'fsdp', axis=0, tiled=True)  407 us
    all_gather x1, waiting for transfers between devices, local(): lax.all_gather(weight_down, 'fsdp', axis=1, tiled=True)  204 us
    ppermute x2, waiting for transfers between devices, ring_gather(): earlier.append(lax.ppermute(earlier[-1], axis, up))  201 us
    ppermute x32, waiting for transfers between devices, from_behind(): lax.ppermute(shard, axis, [(i, (i + by) % peers) for i in range(peers)])  134 us
    reduce_scatter x1, waiting for transfers between devices, local(): lax.psum_scatter(jnp.concatenate([tdot(picked, grad_query_low), tdot(pick...  124 us
    unnamed x136, local copies, waits for them, and re-layouts  76.9 us
  transfers between devices with their start and end apart: 46, of which 39 were waited for; matrix products, arithmetic and copies ran while one was open for 13% of the time, Pallas kernels for 0%

profile of v1, /device:TPU:0, one launch (start us, length us, event | category | flops | bytes accessed | tf_op | source)
XLA Modules:
  0.0 3006.2 jit_solution(16112701161821830357)
XLA Ops:
  9.5 9.5 all-gather
  19.4 45.9 %all-gather.11.cloned.1.call-done = bf16[2048,1024]{1,0:T(8,128)(2,1)} async-done(((bf16[512,1024]{1,0:T(8,128)(2,1)}), bf16[2048,1024]{1,0:T(8,128)(2,1)}) %all-gather.11.cloned.1.call-update) | async-done | bytes 4194320 | tf_op jit(solution)/shard_map/all_gather | solution.py:104
  71.5 9.0 all-reduce.5
  80.8 39.1 %all-gather.15.cloned.1.call-done = bf16[2048,1024]{1,0:T(8,128)(2,1)} async-done(((bf16[512,1024]{1,0:T(8,128)(2,1)}), bf16[2048,1024]{1,0:T(8,128)(2,1)}) %all-gather.15.cloned.1.call-update) | async-done | bytes 4194320 | tf_op jit(solution)/shard_map/all_gather | solution.py:103
  135.8 200.9 %collective-permute-done.4 = bf16[512,6144]{1,0:T(8,128)(2,1)} collective-permute-done((bf16[512,6144]{1,0:T(8,128)(2,1)}, bf16[512,6144]{1,0:T(8,128)(2,1)}, u32[]{:S(2)}, u32[]{:S(2)}) %collective-permute-start.4) | collective-permute-done | bytes 6291488 | tf_op jit(solution)/shard_map/ppermute | solution.py:22
  339.7 407.2 %all-gather.1 = bf16[4,1,512]{2,1,0:T(2,128)(2,1)S(1)} all-gather(bf16[1,1,512]{2,1,0:T(2,128)(2,1)S(1)} %reshape.361), channel_id=1, replica_groups=mesh['ctx'=8,'fsdp'=4] {'fsdp'}, dimensions={0}, use_global_device_ids=true | all-gather | bytes 5120 | tf_op jit(solution)/shard_map/all_gather | solution.py:110
  746.9 12.3 all_gather.42
  760.7 12.2 copy.86
  839.7 15.6 fusion.20
  855.4 14.5 fusion.21
  869.9 15.1 fusion.55
  892.9 19.6 fusion.84
  912.5 203.5 %all-gather.25.cloned.1.call-done = bf16[6144,2048]{1,0:T(8,128)(2,1)} async-done(((bf16[6144,512]{1,0:T(8,128)(2,1)}), bf16[6144,2048]{1,0:T(8,128)(2,1)}) %all-gather.25.cloned.1.call-update) | async-done | bytes 25165840 | tf_op jit(solution)/shard_map/all_gather | solution.py:108
  1116.1 13.8 fusion.59
  1129.8 22.1 multiply_convert_fusion.1
  1152.0 13.5 fusion.85
  1165.4 15.2 multiply_reduce_fusion.1
  1203.1 328.4 %while.24 = (s32[]{:T(128)}, bf16[256,1024]{1,0:T(8,128)(2,1)}, bf16[256,1024]{1,0:T(8,128)(2,1)}, f32[256,1024]{0,1:T(8,128)}, f32[256,1024]{0,1:T(8,128)}, /*i...) while((s32[]{:T(128)}, bf16[256,1024]{1,0:T(8,128)(2,1)}, ...), condition=%wide.region_9.10_spmd.clone, body=%wide.region_8.9_spmd.clone.sunk | while | flops 1355874304 | bytes 68932240 | solution.py:281
  1554.2 18.0 pad_maximum_fusion.1
  1572.3 14.3 convert_bitcast_fusion
  1586.6 14.3 convolution_convert_fusion
  1600.9 14.3 convolution_convert_fusion.1
  1615.2 52.5 %pad_maximum_fusion = bf16[2048,18432]{1,0:T(8,128)(2,1)} fusion(bf16[2048,6144]{1,0:T(8,128)(2,1)} %convert_bitcast_fusion, bf16[2048,6144]{1,0:T(8,128)(2,1)} %convolution_convert_fusion, bf16[2048,6144]{1,0:T(8,128)(2,1)} %convolution_convert_fusion.1), kind=kLoop, calls=%fused_computation.25 | loop fusion | flops 226492416 | bytes 150994944 | tf_op jit(solution)/shard_map/concatenate | solution.py:203
  1667.9 123.6 %reduce-scatter.5.cloned.1.call-done = bf16[512,6144]{0,1:T(8,128)(2,1)} async-done(((bf16[2048,6144]{0,1:T(8,128)(2,1)}), bf16[512,6144]{0,1:T(8,128)(2,1)}) %reduce-scatter.5.cloned.1.call-update) | async-done | bytes 6291472 | tf_op jit(solution)/shard_map/reduce_scatter | solution.py:307
  1791.5 629.2 %reduce-scatter.7.cloned.1.call-done = bf16[512,18432]{1,0:T(8,128)(2,1)} async-done(((bf16[2048,18432]{1,0:T(8,128)(2,1)}), bf16[512,18432]{1,0:T(8,128)(2,1)}) %reduce-scatter.7.cloned.1.call-update) | async-done | bytes 18874384
  2434.2 41.1 %all-reduce.3 = (f32[2048]{0:T(1024)S(1)}, f32[2048]{0:T(1024)S(1)}, f32[128]{0:T(128)S(1)}, f32[128]{0:T(128)S(1)}) all-reduce(f32[2048]{0:T(1024)S(1)} %get-tuple-element.451, f32[2048]{0:T(1024)S(1)} %copy-done.47, f32[128]{0:T(128)S(1)} %get-tuple-element.447, ...), channel_id=1, replica_groups=mesh['ctx'=8,'fsdp'=4] {'ctx','fsdp'}, use_global_device_ids=true, to_apply=%region_18.19 | all-reduce | flops 4352 | bytes 34816 | tf_op jit(solution)/shard_map/psum | solution.py:325
  2482.0 13.7 fusion.41
  2495.7 419.9 %all-reduce.8.cloned.1.call-done = (bf16[512,6144]{0,1:T(8,128)(2,1)}, bf16[512,18432]{1,0:T(8,128)(2,1)}) async-done(((bf16[512,6144]{0,1:T(8,128)(2,1)}, bf16[512,18432]{1,0:T(8,128)(2,1)}), (bf16[512,6144]{0,1:T(8,128)(2,1)}, bf16[512,18432]{1,0:T(8,128)(2,1)})) %all-reduce.8.cloned.1.call-update) | async-done | bytes 25165840 | tf_op jit(solution)/shard_map/psum | solution.py:322
  2915.6 21.3 convert_element_type.227
  2941.1 9.7 fusion.81
  2961.6 10.6 slice_bitcast_fusion
  2972.2 12.6 copy.102
  (500 shorter events, 525.5 us)
Async XLA Ops:
  7.2 58.1 %all-gather.11.cloned.1.call-start = ((), (), s32[]{:S(2)}) async-start(), calls=%async_computation.2 | async-start | bytes 5242880 | tf_op jit(solution)/shard_map/all_gather | solution.py:104
  7.9 112.0 %all-gather.15.cloned.1.call-start = ((), (), s32[]{:S(2)}) async-start(), calls=%async_computation.4 | async-start | bytes 5242880 | tf_op jit(solution)/shard_map/all_gather | solution.py:103
  8.7 752.0 %all-gather.19.cloned.1.call-start = ((), (), s32[]{:S(2)}) async-start(), calls=%async_computation.6 | async-start | bytes 10485760 | tf_op jit(solution)/shard_map/all_gather | solution.py:102
  9.4 823.9 %all-gather.13.cloned.1.call-start = ((), (), s32[]{:S(2)}) async-start(), calls=%async_computation.3 | async-start | bytes 4718592 | tf_op jit(solution)/shard_map/all_gather | solution.py:153
  69.6 770.1 %all-gather.17.cloned.1.call-start = ((), (), s32[]{:S(2)}) async-start(), calls=%async_computation.5 | async-start | bytes 4718592 | tf_op jit(solution)/shard_map/all_gather | solution.py:152
  132.3 754.1 %all-gather.21.cloned.1.call-start = ((), (), s32[]{:S(2)}) async-start(), calls=%async_computation.7 | async-start | bytes 10485760 | tf_op jit(solution)/shard_map/all_gather | solution.py:105
  132.9 760.0 %all-gather.23.cloned.1.call-start = ((), (), s32[]{:S(2)}) async-start(), calls=%async_computation.8 | async-start | bytes 31457280 | tf_op jit(solution)/shard_map/all_gather | solution.py:107
  133.7 982.4 %all-gather.25.cloned.1.call-start = ((), (), s32[]{:S(2)}) async-start(), calls=%async_computation.9 | async-start | bytes 31457280 | tf_op jit(solution)/shard_map/all_gather | solution.py:108
  134.4 1657.0 %reduce-scatter.5.cloned.1.call-start = ((), (), s32[]{:S(2)}) async-start(), calls=%async_computation.10 | async-start | bytes 31457280 | tf_op jit(solution)/shard_map/reduce_scatter | solution.py:307
  134.5 202.3 %collective-permute-start.4 = (bf16[512,6144]{1,0:T(8,128)(2,1)}, bf16[512,6144]{1,0:T(8,128)(2,1)}, u32[]{:S(2)}, u32[]{:S(2)}) collective-permute-start(bf16[512,6144]{1,0:T(8,128)(2,1)} %param.22), channel_id=1, source_target_pairs={{0,1},{1,2},{2,3},{3,0},{4,5},{5,6},{6,7},{7,4},{8,9},{9,10},{10,1... | collective-permute-start | bytes 18874376 | tf_op jit(solution)/shard_map/ppermute | solution.py:22
  336.8 453.0 %collective-permute-start.5 = (bf16[512,6144]{1,0:T(8,128)(2,1)}, bf16[512,6144]{1,0:T(8,128)(2,1)}, u32[]{:S(2)}, u32[]{:S(2)}) collective-permute-start(bf16[512,6144]{1,0:T(8,128)(2,1)} %collective-permute-done.4), channel_id=1, source_target_pairs={{0,1},{1,2},{2,3},{3,0},{4,5},{5,6},{6,7},{7,4},{8,9},{9,10},{10,1... | collective-permute-start | bytes 18874376 | tf_op jit(solution)/shard_map/ppermute | solution.py:22
  336.8 468.7 %collective-permute-start.6 = (bf16[512,6144]{1,0:T(8,128)(2,1)}, bf16[512,6144]{1,0:T(8,128)(2,1)}, u32[]{:S(2)}, u32[]{:S(2)}) collective-permute-start(bf16[512,6144]{1,0:T(8,128)(2,1)} %param.22), channel_id=1, source_target_pairs={{0,3},{1,0},{2,1},{3,2},{4,7},{5,4},{6,5},{7,6},{8,11},{9,8},{10,9... | collective-permute-start | bytes 18874376 | tf_op jit(solution)/shard_map/ppermute | solution.py:24
  1219.0 14.2 collective-permute-start.3
  1220.4 18.3 collective-permute-start
  1220.6 23.8 collective-permute-start.1
  1260.0 19.8 collective-permute-start
  1260.0 25.4 collective-permute-start.1
  1301.0 19.8 collective-permute-start
  1301.0 25.4 collective-permute-start.1
  1342.0 14.2 collective-permute-start.3
  1342.0 19.8 collective-permute-start
  1342.0 25.4 collective-permute-start.1
  1383.0 19.8 collective-permute-start
  1383.0 25.4 collective-permute-start.1
  1424.1 19.8 collective-permute-start
  1424.1 25.4 collective-permute-start.1
  1465.1 19.8 collective-permute-start
  1465.1 25.4 collective-permute-start.1
  1506.1 19.8 collective-permute-start
  1506.1 25.4 collective-permute-start.1
  1572.2 848.5 %reduce-scatter.7.cloned.1.call-start = ((), (), s32[]{:S(2)}) async-start(), calls=%async_computation.11 | async-start | bytes 94371840
  1667.7 1247.9 %all-reduce.8.cloned.1.call-start = ((), (), s32[]{:S(2)}) async-start(), calls=%async_computation.12 | async-start | bytes 50331648 | tf_op jit(solution)/shard_map/psum | solution.py:322
  (111 other events, 7376.0 us)
Sparse Core Ops, SparseCore 0:
  9.9 55.3 all-gather.10
  67.2 52.6 all-gather.14
  121.7 152.0 all-gather.18
  275.2 46.2 all-gather.12
  323.5 46.5 all-gather.16
  371.8 154.1 all-gather.20
  527.8 358.7 all-gather.22
  888.5 227.5 all-gather.24
  1572.3 219.1 reduce-scatter.4
  1794.7 625.8 reduce-scatter.6
  2423.3 492.2 all-reduce.7
